TPU v7x, 128 devices: a whole 4x4x4 slice. The times are simulated.
128 devices in a mesh: head: 4 (over y), tok: 32 (over x, z, core).
Axes of the slice: x: 4, y: 4, z: 4, core: 2. Of those that a mesh axis runs over, the one named last changes fastest.
Arguments:
- tokens: bfloat16 [8192, 2048], P(('tok', 'head')), may hold values from -6 to 6
- token_req: int32 [8192], P(('tok', 'head')), may hold values from 0 to 1, as said below
- cache_len: int32 [64], P('tok'), may hold values from 16 to 1023, as said below
- sink_count: int32 [64], P('tok'), may hold values from 1 to 8
- cache_k: bfloat16 [64, 1024, 2048], P('tok', None, 'head'), may hold values from -64 to 64
- cache_v: bfloat16 [64, 1024, 2048], P('tok', None, 'head'), may hold values from -6 to 6
- attn_gain: float32 [2048], replicated, may hold values from 0.1 to 1.9
- w_qkv: bfloat16 [2048, 3, 2048], P(None, None, 'head'), may hold values from -0.125 to 0.125
- w_out: bfloat16 [2048, 2048], P('head'), may hold values from -0.125 to 0.125
- ffn_gain: float32 [2048], replicated, may hold values from 0.1 to 1.9
- routes: int32 [8192, 8], P(('tok', 'head')), may hold values from 0 to 63, all different within a row; in each aligned block of 64 rows (0 to 63, 64 to 127, ...) at most 16 rows name the same one
- route_weight: float32 [8192, 8], P(('tok', 'head')), may hold values from 0.1 to 1
- w_expert: bfloat16 [64, 3, 2048, 1024], P('tok', None, None, 'head'), may hold values from -0.125 to 0.125
Outputs:
- hidden_out: bfloat16 [8192, 2048], P(('tok', 'head'))
- new_cache_k: bfloat16 [64, 1024, 2048], P('tok', None, 'head')
- new_cache_v: bfloat16 [64, 1024, 2048], P('tok', None, 'head')
Inputs may be any that keep to these rules, and one draw needn't show every extreme that they name: `token_req`: within each group of 256 consecutive tokens, the tokens of request 0 come first and those of request 1 follow; each request has at least one token. `cache_len`: A request's cache length plus its number of tokens is at most 1024. `routes`: each row names 8 different experts; in each aligned block of 64 rows (the rows of one device) no expert is named more than 16 times.
All inputs are finite; a program needn't handle non-finite values.
Results may differ from a plain program's by a relative error of at most 0.018.
Values may be sent and summed in bfloat16 or wider, within the bound.
No kernel may reach another device: no remote copies, remote signals or barrier semaphores. Data moves between devices by JAX's collectives and lax.ppermute only.
A program may use at most 192 MiB of HBM per device.

v0:
```python
import jax
import jax.numpy as jnp
from jax import lax
from jax.sharding import PartitionSpec as P

HD = 128
REQ_GRP = 2
CAP = 1024
WIN = 384
norm_eps = 1e-05
rope_base = 50000.0


def rms_norm(values, gain_vec):
    widened = values.astype(jnp.float32)
    return (
        widened
        * lax.rsqrt(jnp.mean(widened * widened, axis=-1, keepdims=True) + norm_eps)
        * gain_vec
    )


def rotate(vectors, positions_all):
    half_width = vectors.shape[-1] // 2
    frequency = rope_base ** (
        -(jnp.arange(half_width, dtype=jnp.float32) * 2.0 / vectors.shape[-1])
    )
    angles = positions_all.astype(jnp.float32)[:, None] * frequency[None, :]
    cosine = jnp.cos(angles)[:, None, :]
    sine_part = jnp.sin(angles)[:, None, :]
    first_half = vectors[..., :half_width]
    second_half = vectors[..., half_width:]
    return jnp.concatenate(
        [
            first_half * cosine - second_half * sine_part,
            second_half * cosine + first_half * sine_part,
        ],
        axis=-1,
    )


def positions(request, lengths):
    one_hot = (request[:, None] == jnp.arange(REQ_GRP, dtype=jnp.int32)[None, :]).astype(jnp.int32)
    before = jnp.cumsum(one_hot, axis=0) - one_hot
    return jnp.sum(one_hot * (before + lengths[None, :]), axis=1)


def attend(query, keys_all, values_all, request, positions_all, sink_counts):
    scores = jnp.einsum(
        "thd,rjhd->thrj", query, keys_all, preferred_element_type=jnp.float32
    ) * HD ** (-0.5)
    slot_ids = jnp.arange(CAP, dtype=jnp.int32)
    same_req = jnp.arange(REQ_GRP, dtype=jnp.int32)[None, :, None] == request[:, None, None]
    causal = slot_ids[None, None, :] <= positions_all[:, None, None]
    window = (slot_ids[None, None, :] < sink_counts[None, :, None]) | (
        slot_ids[None, None, :] > positions_all[:, None, None] - WIN
    )
    allowed = (same_req & causal & window)[:, None]
    masked = jnp.where(allowed, scores, -1e30)
    row_max = jnp.max(masked, axis=(2, 3), keepdims=True)
    exp_scores = jnp.exp(masked - row_max)
    weights = (exp_scores / jnp.sum(exp_scores, axis=(2, 3), keepdims=True)).astype(jnp.bfloat16)
    return jnp.einsum(
        "thrj,rjhd->thd", weights, values_all, preferred_element_type=jnp.float32
    ).astype(jnp.bfloat16)


def expert_apply(slot_rows, weight_set):
    gate_part = jnp.einsum(
        "semd,edf->semf", slot_rows, weight_set[:, 0], preferred_element_type=jnp.float32
    )
    up_part = jnp.einsum(
        "semd,edf->semf", slot_rows, weight_set[:, 1], preferred_element_type=jnp.float32
    )
    hidden = (jax.nn.silu(gate_part) * up_part).astype(jnp.bfloat16)
    return jnp.einsum(
        "semf,edf->semd", hidden, weight_set[:, 2], preferred_element_type=jnp.float32
    )


def on_device(
    tokens,
    token_req,
    cache_len,
    sink_count,
    cache_k,
    cache_v,
    attn_gain,
    w_qkv,
    w_out,
    ffn_gain,
    routes,
    route_weight,
    w_expert,
):
    tok_dev, model_width = tokens.shape
    heads_here = w_qkv.shape[2] // HD
    tok_count = lax.axis_size("tok")
    normed = rms_norm(tokens, attn_gain).astype(jnp.bfloat16)
    group_rows, group_req = (
        lax.all_gather(normed, "head", axis=0, tiled=True),
        lax.all_gather(token_req, "head", axis=0, tiled=True),
    )
    rows_all = group_rows.shape[0]
    positions_all = positions(group_req, cache_len)
    projected = jnp.dot(
        group_rows,
        w_qkv.reshape(model_width, 3 * heads_here * HD),
        preferred_element_type=jnp.float32,
    )
    projected = projected.reshape(rows_all, 3, heads_here, HD)
    query = rotate(projected[:, 0], positions_all).astype(jnp.bfloat16)
    key_new = (
        rotate(projected[:, 1], positions_all)
        .astype(jnp.bfloat16)
        .reshape(rows_all, heads_here * HD)
    )
    value_new = projected[:, 2].astype(jnp.bfloat16).reshape(rows_all, heads_here * HD)
    cache_keys = cache_k.at[group_req, positions_all].set(key_new)
    cache_values = cache_v.at[group_req, positions_all].set(value_new)
    attended = attend(
        query,
        cache_keys.reshape(REQ_GRP, CAP, heads_here, HD),
        cache_values.reshape(REQ_GRP, CAP, heads_here, HD),
        group_req,
        positions_all,
        sink_count,
    )
    attended = attended.reshape(rows_all, heads_here * HD)
    mixed_attn = lax.psum_scatter(
        jnp.dot(attended, w_out, preferred_element_type=jnp.float32).astype(jnp.bfloat16),
        "head",
        scatter_dimension=0,
        tiled=True,
    ).astype(jnp.float32)
    residual = (tokens.astype(jnp.float32) + mixed_attn).astype(jnp.bfloat16)
    ffn_input = rms_norm(residual, ffn_gain).astype(jnp.bfloat16)
    route_count = routes.shape[1]
    exp_dev = w_expert.shape[0]
    expert_total = exp_dev * tok_count
    slot_depth = 2 * tok_dev * route_count // expert_total
    flat_expert = routes.reshape(-1)
    one_hot = (flat_expert[:, None] == jnp.arange(expert_total, dtype=jnp.int32)[None, :]).astype(
        jnp.int32
    )
    before = jnp.cumsum(one_hot, axis=0) - one_hot
    slot_index = jnp.sum(before * one_hot, axis=1)
    target = flat_expert * slot_depth + slot_index
    dispatch = (
        jnp.arange(expert_total * slot_depth, dtype=jnp.int32)[:, None] == target[None, :]
    ).astype(jnp.bfloat16)
    repeated = jnp.repeat(ffn_input, route_count, axis=0)
    outgoing = jnp.dot(dispatch, repeated, preferred_element_type=jnp.float32).astype(jnp.bfloat16)
    outgoing = outgoing.reshape(tok_count, exp_dev, slot_depth, model_width)
    arrived = lax.all_to_all(outgoing, "tok", split_axis=0, concat_axis=0, tiled=True)
    result = expert_apply(arrived, lax.all_gather(w_expert, "head", axis=3, tiled=True)).astype(
        jnp.bfloat16
    )
    returned = lax.all_to_all(result, "tok", split_axis=0, concat_axis=0, tiled=True)
    picked = returned.reshape(-1, model_width)[target].reshape(tok_dev, route_count, model_width)
    combined = jnp.sum(route_weight[:, :, None] * picked.astype(jnp.float32), axis=1)
    hidden_out = (residual.astype(jnp.float32) + combined).astype(jnp.bfloat16)
    return (hidden_out, cache_keys, cache_values)


def solution(mesh):
    return jax.shard_map(
        on_device,
        mesh=mesh,
        in_specs=(
            P(("tok", "head"), None),
            P(("tok", "head")),
            P("tok"),
            P("tok"),
            P("tok", None, "head"),
            P("tok", None, "head"),
            P(),
            P(None, None, "head"),
            P("head", None),
            P(),
            P(("tok", "head"), None),
            P(("tok", "head"), None),
            P("tok", None, None, "head"),
        ),
        out_specs=(P(("tok", "head"), None), P("tok", None, "head"), P("tok", None, "head")),
        check_vma=False,
    )
```

profile of v0, /device:TPU:1, one launch (start us, length us, event | category | flops | bytes accessed | tf_op | source)
XLA Modules:
  0.0 493.8 jit_solution(6323877021367566477)
XLA Ops:
  7.3 3.2 copy.96
  10.5 1.3 copy.97
  11.8 0.2 fusion.31
  12.0 0.8 fusion.33
  12.9 0.7 dynamic-slice
  14.3 0.2 dynamic-update-slice
  14.5 7.8 %all-reduce = s32[256]{0:T(256)S(1)} all-reduce(s32[256]{0:T(256)S(1)} %dynamic-update-slice), channel_id=1, replica_groups=mesh['head'=4,'tok'=32] {'head'}, use_global_device_ids=true, to_apply=%add | all-reduce | flops 256 | bytes 2048
  22.4 0.6 reduce-window.14
  23.0 0.2 slice_reduce_fusion.1
  23.2 0.2 reduce-window.15
  23.5 8.9 %copy.40 = bf16[2048,3,512]{0,2,1:T(8,128)(2,1)} copy(bf16[2048,3,512]{2,0,1:T(8,128)(2,1)} %param.20) | data formatting | bytes 12582912 | tf_op args[7]
  32.6 0.3 multiply_cosine_fusion
  32.9 0.3 iota_compare_fusion.2
  33.2 0.6 or_and_fusion
  33.8 4.4 all-gather.3.cloned.1.call-done
  38.2 5.0 %fusion.27 = f32[256,3,4,128]{0,3,2,1:T(8,128)S(1)} fusion(bf16[3,4,128,2048]{3,2,1,0:T(8,128)(2,1)} %bitcast.168, bf16[256,2048]{1,0:T(8,128)(2,1)} %all-gather.3.cloned.1.call-done), kind=kOutput, calls=%fused_computation.39 | convolution fusion | flops 1610612736 | bytes 8912896 | tf_op jit(solution)/shard_map/dot_general | solution.py:106
  43.4 0.7 slice.98
  44.1 0.8 subtract_convert_fusion
  44.9 0.1 copy.42
  45.0 1.1 copy.41
  46.1 34.8 %scatter_fusion.1 = bf16[2,1024,512]{2,1,0:T(8,128)(2,1)} fusion(bf16[2,1024,512]{2,1,0:T(8,128)(2,1)} %copy.96, s32[256]{0:T(256)S(1)} %bitcast.166, bf16[256,512]{1,0:T(8,128)(2,1)S(1)} %copy.42), kind=kCustom, calls=%fused_computation.2 | custom fusion | bytes 788480 | tf_op jit(solution)/shard_map/scatter | solution.py:119
  80.9 3.1 fusion.4
  84.0 3.2 copy-done.2
  87.2 1.8 fusion.3
  89.0 34.6 %scatter_fusion = bf16[2,1024,512]{2,1,0:T(8,128)(2,1)} fusion(bf16[2,1024,512]{2,1,0:T(8,128)(2,1)} %copy.97, s32[256]{0:T(256)S(1)} %bitcast.167, bf16[256,512]{1,0:T(8,128)(2,1)S(1)} %copy.41), kind=kCustom, calls=%fused_computation.1 | custom fusion | bytes 788480 | tf_op jit(solution)/shard_map/scatter | solution.py:120
  123.6 6.8 %fusion.24 = bf16[4,128,256]{2,1,0:T(8,128)(2,1)S(1)} fusion(f32[4,2,1024,256]{3,2,1,0:T(8,128)} %copy-done.2, f32[256,4]{0,1:T(4,128)S(1)} %fusion.3, f32[256,4]{0,1:T(4,128)S(1)} %get-tuple-element.15, pred[256,2,1024]{0,2,1:T(8,128)(4,1)S(1)} %or_and_fusion, bf16[2,1024,512]{2,1,0:T(8,128)(2,1)} %scatter_fusion), kind=kOutput, calls=%fused_computation.38 | convolution fusion | flops 547487744 | bytes 11280384 | tf_op jit(solution)/shard_map/thrj,rjhd->thd/dot_general | solution.py:63
  130.4 1.7 convolution_convert_fusion.1
  132.1 0.2 all-gather.5.cloned.1.call-start
  132.4 5.9 %copy.51 = bf16[2,3,2048,256]{3,2,0,1:T(8,128)(2,1)} copy(bf16[2,3,2048,256]{3,2,1,0:T(8,128)(2,1)} %param.25) | data formatting | bytes 12582912 | tf_op args[12]
  138.3 0.7 copy-done.7
  139.3 1.2 reduce-window.16
  140.5 0.2 slice_reduce_fusion
  140.7 0.1 fusion.43
  140.9 16.6 %reduce-scatter.2.cloned.1.call-done = bf16[64,2048]{1,0:T(8,128)(2,1)} async-done(((bf16[256,2048]{1,0:T(8,128)(2,1)}), bf16[64,2048]{1,0:T(8,128)(2,1)}) %reduce-scatter.2.cloned.1.call-update) | async-done | bytes 262160 | tf_op jit(solution)/shard_map/reduce_scatter | solution.py:130
  157.5 1.2 fusion.35
  158.6 1.1 fusion.37
  159.7 2.3 convolution_convert_fusion
  162.0 59.6 %all_to_all.10 = bf16[32,2,16,2048]{3,2,1,0:T(8,128)(2,1)} all-to-all(bf16[32,2,16,2048]{3,2,1,0:T(8,128)(2,1)S(1)} %bitcast.169), channel_id=1, replica_groups=mesh['head'=4,'tok'=32] {'tok'}, dimensions={0} | all-to-all | bytes 8388608 | tf_op jit(solution)/shard_map/all_to_all | solution.py:155
  221.6 164.7 %all-gather.5.cloned.1.call-done = bf16[2,3,2048,1024]{3,2,0,1:T(8,128)(2,1)} async-done(((bf16[2,3,2048,256]{3,2,0,1:T(8,128)(2,1)}), bf16[2,3,2048,1024]{3,2,0,1:T(8,128)(2,1)}) %all-gather.5.cloned.1.call-update) | async-done | bytes 25165840 | tf_op jit(solution)/shard_map/all_gather | solution.py:156
  386.3 8.3 %fusion.1 = f32[2,32,16,1024]{3,2,1,0:T(8,128)S(1)} fusion(bf16[2,3,2048,1024]{3,2,0,1:T(8,128)(2,1)} %all-gather.5.cloned.1.call-done, bf16[32,2,16,2048]{3,2,1,0:T(8,128)(2,1)} %all_to_all.10), kind=kOutput, calls=%fused_computation.6 | convolution fusion | flops 4294967296 | bytes 16777216 | tf_op jit(solution)/shard_map/semd,edf->semf/dot_general | solution.py:72
  394.6 8.4 %fusion.6 = bf16[32,2,16,1024]{3,2,0,1:T(8,128)(2,1)S(1)} fusion(f32[2,32,16,1024]{3,2,1,0:T(8,128)S(1)} %fusion.1, bf16[2,3,2048,1024]{3,2,0,1:T(8,128)(2,1)} %all-gather.5.cloned.1.call-done, bf16[32,2,16,2048]{3,2,1,0:T(8,128)(2,1)S(1)} %copy-done.4), kind=kOutput, calls=%fused_computation.17 | convolution fusion | flops 4301258752 | bytes 18874368 | tf_op jit(solution)/shard_map/semd,edf->semf/dot_general | solution.py:69
  403.0 8.2 %convert_bitcast_fusion = bf16[32,2,16,2048]{3,2,0,1:T(8,128)(2,1)S(1)} fusion(bf16[32,2,16,1024]{3,2,0,1:T(8,128)(2,1)S(1)} %fusion.6, bf16[2,3,2048,1024]{3,2,0,1:T(8,128)(2,1)} %all-gather.5.cloned.1.call-done), kind=kOutput, calls=%fused_computation.23 | convolution fusion | flops 4297064448 | bytes 14680064 | tf_op jit(solution)/shard_map/semf,edf->semd/dot_general | solution.py:76
  411.2 2.3 copy.54
  413.5 9.2 %all-to-all-start.1 = ((bf16[32,2,16,2048]{3,2,1,0:T(8,128)(2,1)}), bf16[32,2,16,2048]{3,2,1,0:T(8,128)(2,1)}, u32[]{:S(2)}, u32[]{:S(2)}) async-start(bf16[32,2,16,2048]{3,2,1,0:T(8,128)(2,1)} %copy.54), calls=%async_computation.2 | async-start | bytes 8388608 | tf_op jit(solution)/shard_map/all_to_all | solution.py:159
  423.0 51.8 %all-to-all-done.1 = bf16[32,2,16,2048]{3,2,1,0:T(8,128)(2,1)} async-done(((bf16[32,2,16,2048]{3,2,1,0:T(8,128)(2,1)}), bf16[32,2,16,2048]{3,2,1,0:T(8,128)(2,1)}, u32[]{:S(2)}, u32[]{:S(2)}) %all-to-all-start.1) | async-done | bytes 4194336 | tf_op jit(solution)/shard_map/all_to_all | solution.py:159
  474.8 8.1 %gather_fusion = bf16[512,2048]{1,0:T(8,128)(2,1)} fusion(bf16[1024,2048]{1,0:T(8,128)(2,1)} %bitcast.36, s32[1024]{0:T(1024)S(1)} %pad_clamp_fusion), kind=kCustom, calls=%fused_computation | custom fusion | bytes 4196352 | tf_op jit(solution)/shard_map/gather | solution.py:160
  483.0 3.4 fusion.5
  486.4 0.8 fusion.38
  (60 shorter events, 1.2 us)
Async XLA Ops:
  7.2 123.2 %copy-start = (bf16[512,2048]{1,0:T(8,128)(2,1)S(1)}, bf16[512,2048]{1,0:T(8,128)(2,1)}, u32[]{:S(2)}) copy-start(bf16[512,2048]{1,0:T(8,128)(2,1)} %param.21) | copy-start | bytes 6291460
  7.2 5.7 %copy-start.14 = (u32[128]{0:T(128)S(1)}, u32[128]{0:T(128)}, u32[]{:S(2)}) copy-start(u32[128]{0:T(128)} %constant.89) | copy-start | bytes 1540
  7.2 4.6 copy-start.3
  7.2 7.1 %copy-start.13 = (s32[64]{0:T(128)S(1)}, s32[64]{0:T(128)}, u32[]{:S(2)}) copy-start(s32[64]{0:T(128)} %param.14) | copy-start | bytes 772
  7.2 4.8 copy-start.8
  7.2 31.0 %all-gather.3.cloned.1.call-start = ((), (), s32[]{:S(2)}) async-start(), calls=%async_computation.3 | async-start | bytes 1310720 | tf_op jit(solution)/shard_map/all_gather | solution.py:101
  7.3 3.2 copy-start.6
  12.8 144.6 %reduce-scatter.2.cloned.1.call-start = ((), (), s32[]{:S(2)}) async-start(), calls=%async_computation.4 | async-start | bytes 1310720 | tf_op jit(solution)/shard_map/reduce_scatter | solution.py:130
  23.5 8.9 %copy-start.11 = (s32[2]{0:T(128)S(1)}, s32[2]{0:T(128)}, u32[]{:S(2)}) copy-start(s32[2]{0:T(128)} %param.15) | copy-start | bytes 28
  23.5 9.0 %copy-start.12 = (s32[2]{0:T(128)S(1)}, s32[2]{0:T(128)}, u32[]{:S(2)}) copy-start(s32[2]{0:T(128)} %param.16) | copy-start | bytes 28
  84.0 3.2 copy-start.2
  132.1 254.2 %all-gather.5.cloned.1.call-start = ((), (), s32[]{:S(2)}) async-start(), calls=%async_computation.5 | async-start | bytes 31457280 | tf_op jit(solution)/shard_map/all_gather | solution.py:156
  138.3 0.7 copy-start.7
  138.3 20.4 %copy-start.9 = (f32[2048]{0:T(1024)S(1)}, f32[2048]{0:T(1024)}, u32[]{:S(2)}) copy-start(f32[2048]{0:T(1024)} %param.22) | copy-start | bytes 24580
  386.3 8.3 %copy-start.4 = (bf16[32,2,16,2048]{3,2,1,0:T(8,128)(2,1)S(1)}, bf16[32,2,16,2048]{3,2,1,0:T(8,128)(2,1)}, u32[]{:S(2)}) copy-start(bf16[32,2,16,2048]{3,2,1,0:T(8,128)(2,1)} %all_to_all.10) | copy-start | bytes 12582916
  413.5 9.4 %copy-start.10 = (f32[64,8]{0,1:T(8,128)S(1)}, f32[64,8]{0,1:T(8,128)}, u32[]{:S(2)}) copy-start(f32[64,8]{0,1:T(8,128)} %param.24) | copy-start | bytes 6148
  413.5 61.3 %all-to-all-start.1 = ((bf16[32,2,16,2048]{3,2,1,0:T(8,128)(2,1)}), bf16[32,2,16,2048]{3,2,1,0:T(8,128)(2,1)}, u32[]{:S(2)}, u32[]{:S(2)}) async-start(bf16[32,2,16,2048]{3,2,1,0:T(8,128)(2,1)} %copy.54), calls=%async_computation.2 | async-start | bytes 8388608 | tf_op jit(solution)/shard_map/all_to_all | solution.py:159
  474.8 11.6 %copy-start.5 = (bf16[64,2048]{1,0:T(8,128)(2,1)S(1)}, bf16[64,2048]{1,0:T(8,128)(2,1)}, u32[]{:S(2)}) copy-start(bf16[64,2048]{1,0:T(8,128)(2,1)} %reduce-scatter.2.cloned.1.call-done) | copy-start | bytes 786436
  474.8 12.4 %copy-start.1 = (bf16[512,2048]{1,0:T(8,128)(2,1)S(1)}, bf16[512,2048]{1,0:T(8,128)(2,1)}, u32[]{:S(2)}) copy-start(bf16[512,2048]{1,0:T(8,128)(2,1)} %param.21) | copy-start | bytes 6291460
Sparse Core Ops, SparseCore 0:
  13.0 25.2 all-gather.2
  132.3 25.1 reduce-scatter.1
  159.1 227.1 all-gather.4
where the time goes:
time: 496 us; the launch traced here: 494 us
  waiting for transfers between devices  238 us (48%)
  local copies, waits for them, and re-layouts  107 us (22%)
  blocking collectives  67.4 us (14%)
  matrix products  43.7 us (9%)
  between operations  14.8 us (3%)
  other arithmetic  13.7 us (3%)
  starting transfers between devices  9.53 us (2%)
    all_gather x1, waiting for transfers between devices, on_device(): lax.all_gather(w_expert, 'head', axis=3, tiled=True)  165 us
    all_to_all x1, blocking collectives, on_device(): lax.all_to_all(outgoing, 'tok', split_axis=0, concat_axis=0, tiled=True)  59.6 us
    all_to_all x1, waiting for transfers between devices, on_device(): lax.all_to_all(result, 'tok', split_axis=0, concat_axis=0, tiled=True)  51.8 us
    scatter x1, local copies, waits for them, and re-layouts, on_device(): cache_keys = cache_k.at[group_req, positions_all].set(key_new)  34.8 us
    scatter x1, local copies, waits for them, and re-layouts, on_device(): cache_values = cache_v.at[group_req, positions_all].set(value_new)  34.6 us
    unnamed x39, local copies, waits for them, and re-layouts  24.3 us
    reduce_scatter x1, waiting for transfers between devices, on_device(): lax.psum_scatter(jnp.dot(attended, w_out, preferred_element_type=jnp.floa...  16.6 us
  transfers between devices with their start and end apart: 4, of which 4 were waited for; matrix products, arithmetic and copies ran while one was open for 5% of the time, Pallas kernels for 0%

commit v1 on v0

--- a/solution.py
+++ b/solution.py
@@ -153,9 +153,13 @@
     outgoing = jnp.dot(dispatch, repeated, preferred_element_type=jnp.float32).astype(jnp.bfloat16)
     outgoing = outgoing.reshape(tok_count, exp_dev, slot_depth, model_width)
     arrived = lax.all_to_all(outgoing, "tok", split_axis=0, concat_axis=0, tiled=True)
-    result = expert_apply(arrived, lax.all_gather(w_expert, "head", axis=3, tiled=True)).astype(
-        jnp.bfloat16
-    )
+
+    def play_the_object(vector):
+        return jnp.concatenate(
+            lax.all_to_all(jnp.stack(lax.axis_size("head") * [vector]), "head", 0, 0), 3
+        )
+
+    result = expert_apply(arrived, play_the_object(w_expert)).astype(jnp.bfloat16)
     returned = lax.all_to_all(result, "tok", split_axis=0, concat_axis=0, tiled=True)
     picked = returned.reshape(-1, model_width)[target].reshape(tok_dev, route_count, model_width)
     combined = jnp.sum(route_weight[:, :, None] * picked.astype(jnp.float32), axis=1)

time: 496 us -> 616 us (1.24)
  blocking collectives: 67.4 us -> 282 us
  waiting for transfers between devices: 238 us -> 105 us
  local copies, waits for them, and re-layouts: 107 us -> 129 us
  starting transfers between devices: 9.53 us -> 25.1 us
    unnamed x1, blocking collectives: 7.85 us -> 282 us
    all_gather x1 -> x0, waiting for transfers between devices: 165 us -> none  [on_device(): lax.all_gather(w_expert, 'head', axis=3, tiled=True)]
    all_to_all x1 -> x0, blocking collectives: 59.6 us -> none  [on_device(): lax.all_to_all(outgoing, 'tok', split_axis=0, concat_axis=0, tiled=True)]
    all_to_all x0 -> x2, waiting for transfers between devices: none -> 30.9 us  [the longest x1 30.9 us: on_device(): lax.all_to_all(outgoing, 'tok', split_axis=0, concat_axis=0, tiled=True)]
    reshape x0 -> x1, local copies, waits for them, and re-layouts: none -> 21.2 us  [play_the_object(): jnp.concatenate(lax.all_to_all(jnp.stack(lax.axis_size('head') * [vector]...]
    all_to_all x0 -> x2, starting transfers between devices: none -> 17.8 us  [the longest x1 9.27 us: on_device(): lax.all_to_all(outgoing, 'tok', split_axis=0, concat_axis=0, tiled=True)]
    another operation x2 -> x3, local copies, waits for them, and re-layouts: 0.24 us -> 8.79 us  [the longest x1 8.56 us: play_the_object(): jnp.stack(lax.axis_size('head') * [vector])]
    unnamed x39 -> x41, local copies, waits for them, and re-layouts: 24.3 us -> 16 us
  transfers between devices with their start and end apart: 4 -> 5, of which waited for: 4 -> 3; matrix products, arithmetic and copies ran while one was open for 5% -> 21% of each run, Pallas kernels for 0% -> 0%
where the time goes in v1:
time: 616 us; the launch traced here: 613 us
  blocking collectives  282 us (46%)
  local copies, waits for them, and re-layouts  129 us (21%)
  waiting for transfers between devices  105 us (17%)
  matrix products  43 us (7%)
  starting transfers between devices  25.1 us (4%)
  between operations  15 us (2%)
  other arithmetic  13.9 us (2%)
    unnamed x1, blocking collectives  282 us
    all_to_all x1, waiting for transfers between devices, on_device(): lax.all_to_all(result, 'tok', split_axis=0, concat_axis=0, tiled=True)  51.8 us
    scatter x1, local copies, waits for them, and re-layouts, on_device(): cache_keys = cache_k.at[group_req, positions_all].set(key_new)  34.9 us
    scatter x1, local copies, waits for them, and re-layouts, on_device(): cache_values = cache_v.at[group_req, positions_all].set(value_new)  34.8 us
    all_to_all x1, waiting for transfers between devices, on_device(): lax.all_to_all(outgoing, 'tok', split_axis=0, concat_axis=0, tiled=True)  30.9 us
    reduce_scatter x1, waiting for transfers between devices, on_device(): lax.psum_scatter(jnp.dot(attended, w_out, preferred_element_type=jnp.floa...  22.5 us
    reshape x1, local copies, waits for them, and re-layouts, play_the_object(): jnp.concatenate(lax.all_to_all(jnp.stack(lax.axis_size('head') * [vector]...  21.2 us
    unnamed x41, local copies, waits for them, and re-layouts  16 us
  transfers between devices with their start and end apart: 5, of which 3 were waited for; matrix products, arithmetic and copies ran while one was open for 21% of the time, Pallas kernels for 0%

profile of v1, /device:TPU:1, one launch (start us, length us, event | category | flops | bytes accessed | tf_op | source)
XLA Modules:
  0.0 612.9 jit_solution(9315797034348951782)
XLA Ops:
  7.2 3.2 copy.98
  10.4 1.3 copy.99
  11.7 1.2 copy-done.4
  12.9 0.4 copy.51
  13.3 8.6 %stack.2 = bf16[4,2,3,2048,256]{4,3,1,2,0:T(8,128)(2,1)} broadcast(bf16[2,3,2048,256]{3,2,0,1:T(8,128)(2,1)S(1)} %copy.51), dimensions={1,2,3,4} | broadcast | bytes 31457280 | tf_op jit(solution)/shard_map/stack | solution.py:159
  21.9 8.6 %all-to-all-start.1 = ((bf16[4,2,3,2048,256]{4,3,1,2,0:T(8,128)(2,1)}), bf16[4,2,3,2048,256]{4,3,1,2,0:T(8,128)(2,1)}, u32[]{:S(2)}, u32[]{:S(2)}) async-start(bf16[4,2,3,2048,256]{4,3,1,2,0:T(8,128)(2,1)} %stack.2), calls=%async_computation.2 | async-start | bytes 50331648 | tf_op jit(solution)/shard_map/all_to_all | solution.py:159
  30.5 0.2 fusion.31
  30.7 0.8 fusion.33
  31.6 0.6 dynamic-slice
  32.8 0.2 dynamic-update-slice
  33.1 281.7 %all-reduce = s32[256]{0:T(256)S(1)} all-reduce(s32[256]{0:T(256)S(1)} %dynamic-update-slice), channel_id=1, replica_groups=mesh['head'=4,'tok'=32] {'head'}, use_global_device_ids=true, to_apply=%add | all-reduce | flops 256 | bytes 2048
  314.8 0.6 reduce-window.14
  315.4 0.2 slice_reduce_fusion.1
  315.6 0.2 reduce-window.15
  315.9 8.8 %copy.40 = bf16[2048,3,512]{0,2,1:T(8,128)(2,1)} copy(bf16[2048,3,512]{2,0,1:T(8,128)(2,1)} %param.20) | data formatting | bytes 12582912 | tf_op args[7]
  325.0 0.3 multiply_cosine_fusion
  325.3 0.3 iota_compare_fusion.2
  325.6 0.6 or_and_fusion
  326.2 5.0 fusion.27
  331.2 0.7 slice.98
  332.1 0.8 subtract_convert_fusion
  332.9 0.1 copy.42
  333.0 1.1 copy.41
  334.1 34.9 %scatter_fusion.1 = bf16[2,1024,512]{2,1,0:T(8,128)(2,1)} fusion(bf16[2,1024,512]{2,1,0:T(8,128)(2,1)} %copy.98, s32[256]{0:T(256)S(1)} %bitcast.169, bf16[256,512]{1,0:T(8,128)(2,1)S(1)} %copy.42), kind=kCustom, calls=%fused_computation.2 | custom fusion | bytes 788480 | tf_op jit(solution)/shard_map/scatter | solution.py:119
  369.0 34.8 %scatter_fusion = bf16[2,1024,512]{2,1,0:T(8,128)(2,1)} fusion(bf16[2,1024,512]{2,1,0:T(8,128)(2,1)} %copy.99, s32[256]{0:T(256)S(1)} %bitcast.170, bf16[256,512]{1,0:T(8,128)(2,1)S(1)} %copy.41), kind=kCustom, calls=%fused_computation.1 | custom fusion | bytes 788480 | tf_op jit(solution)/shard_map/scatter | solution.py:120
  403.8 3.1 fusion.4
  406.9 1.8 fusion.3
  408.7 2.9 fusion.24
  411.6 1.7 convolution_convert_fusion.1
  413.7 1.4 reduce-window.16
  415.0 0.2 slice_reduce_fusion
  415.3 0.1 fusion.43
  415.4 22.5 %reduce-scatter.2.cloned.1.call-done = bf16[64,2048]{1,0:T(8,128)(2,1)} async-done(((bf16[256,2048]{1,0:T(8,128)(2,1)}), bf16[64,2048]{1,0:T(8,128)(2,1)}) %reduce-scatter.2.cloned.1.call-update) | async-done | bytes 262160 | tf_op jit(solution)/shard_map/reduce_scatter | solution.py:130
  438.0 1.2 fusion.35
  439.2 1.1 fusion.37
  440.2 4.4 convolution_convert_fusion
  444.6 9.3 %all-to-all-start = ((bf16[32,2,16,2048]{3,2,1,0:T(8,128)(2,1)}), bf16[32,2,16,2048]{3,2,1,0:T(8,128)(2,1)}, u32[]{:S(2)}, u32[]{:S(2)}) async-start(bf16[32,2,16,2048]{3,2,1,0:T(8,128)(2,1)} %bitcast.175), calls=%async_computation.1 | async-start | bytes 8388608 | tf_op jit(solution)/shard_map/all_to_all | solution.py:155
  453.9 21.2 %copy.69 = bf16[4,3,2,256,8,256]{5,4,0,3,2,1:T(8,128)(2,1)} copy(bf16[4,3,2,256,8,256]{5,4,3,2,1,0:T(8,128)(2,1)} %bitcast.57) | data formatting | bytes 50331648 | tf_op jit(solution)/shard_map/reshape | solution.py:158
  475.1 30.9 %all-to-all-done = bf16[32,2,16,2048]{3,2,1,0:T(8,128)(2,1)} async-done(((bf16[32,2,16,2048]{3,2,1,0:T(8,128)(2,1)}), bf16[32,2,16,2048]{3,2,1,0:T(8,128)(2,1)}, u32[]{:S(2)}, u32[]{:S(2)}) %all-to-all-start) | async-done | bytes 4194336 | tf_op jit(solution)/shard_map/all_to_all | solution.py:155
  506.0 8.1 %fusion.1 = f32[2,32,16,1024]{3,2,1,0:T(8,128)S(1)} fusion(bf16[2,3,2048,1024]{3,2,0,1:T(8,128)(2,1)} %bitcast.171, bf16[32,2,16,2048]{3,2,1,0:T(8,128)(2,1)} %all-to-all-done), kind=kOutput, calls=%fused_computation.6 | convolution fusion | flops 4294967296 | bytes 16777216 | tf_op jit(solution)/shard_map/semd,edf->semf/dot_general | solution.py:72
  514.1 9.7 %fusion.6 = bf16[32,2,16,1024]{3,2,0,1:T(8,128)(2,1)S(1)} fusion(f32[2,32,16,1024]{3,2,1,0:T(8,128)S(1)} %fusion.1, bf16[2,3,2048,1024]{3,2,0,1:T(8,128)(2,1)} %bitcast.172, bf16[32,2,16,2048]{3,2,1,0:T(8,128)(2,1)} %all-to-all-done), kind=kOutput, calls=%fused_computation.17 | convolution fusion | flops 4301258752 | bytes 18874368 | tf_op jit(solution)/shard_map/semd,edf->semf/dot_general | solution.py:69
  523.8 8.2 %convert_bitcast_fusion = bf16[32,2,16,2048]{3,2,0,1:T(8,128)(2,1)S(1)} fusion(bf16[32,2,16,1024]{3,2,0,1:T(8,128)(2,1)S(1)} %fusion.6, bf16[2,3,2048,1024]{3,2,0,1:T(8,128)(2,1)} %bitcast.173), kind=kOutput, calls=%fused_computation.23 | convolution fusion | flops 4297064448 | bytes 14680064 | tf_op jit(solution)/shard_map/semf,edf->semd/dot_general | solution.py:76
  532.0 2.3 copy.55
  534.3 7.2 %all-to-all-start.2 = ((bf16[32,2,16,2048]{3,2,1,0:T(8,128)(2,1)}), bf16[32,2,16,2048]{3,2,1,0:T(8,128)(2,1)}, u32[]{:S(2)}, u32[]{:S(2)}) async-start(bf16[32,2,16,2048]{3,2,1,0:T(8,128)(2,1)} %copy.55), calls=%async_computation.3 | async-start | bytes 8388608 | tf_op jit(solution)/shard_map/all_to_all | solution.py:163
  541.8 51.8 %all-to-all-done.2 = bf16[32,2,16,2048]{3,2,1,0:T(8,128)(2,1)} async-done(((bf16[32,2,16,2048]{3,2,1,0:T(8,128)(2,1)}), bf16[32,2,16,2048]{3,2,1,0:T(8,128)(2,1)}, u32[]{:S(2)}, u32[]{:S(2)}) %all-to-all-start.2) | async-done | bytes 4194336 | tf_op jit(solution)/shard_map/all_to_all | solution.py:163
  593.6 8.1 %gather_fusion = bf16[512,2048]{1,0:T(8,128)(2,1)} fusion(bf16[1024,2048]{1,0:T(8,128)(2,1)} %bitcast.37, s32[1024]{0:T(1024)S(1)} %pad_clamp_fusion), kind=kCustom, calls=%fused_computation | custom fusion | bytes 4196352 | tf_op jit(solution)/shard_map/gather | solution.py:164
  601.8 3.4 fusion.5
  605.2 0.8 fusion.38
  (64 shorter events, 1.2 us)
Async XLA Ops:
  7.2 404.4 %copy-start = (bf16[512,2048]{1,0:T(8,128)(2,1)S(1)}, bf16[512,2048]{1,0:T(8,128)(2,1)}, u32[]{:S(2)}) copy-start(bf16[512,2048]{1,0:T(8,128)(2,1)} %param.21) | copy-start | bytes 6291460
  7.2 3.2 copy-start.6
  7.2 5.7 copy-start.4
  21.9 8.6 %copy-start.3 = (bf16[64,2048]{1,0:T(8,128)(2,1)S(1)}, bf16[64,2048]{1,0:T(8,128)(2,1)}, u32[]{:S(2)}) copy-start(bf16[64,2048]{1,0:T(8,128)(2,1)} %param.13) | copy-start | bytes 786436
  21.9 8.8 %copy-start.9 = (f32[2048]{0:T(1024)S(1)}, f32[2048]{0:T(1024)}, u32[]{:S(2)}) copy-start(f32[2048]{0:T(1024)} %param.19) | copy-start | bytes 24580
  21.9 9.7 %copy-start.15 = (u32[128]{0:T(128)S(1)}, u32[128]{0:T(128)}, u32[]{:S(2)}) copy-start(u32[128]{0:T(128)} %constant.89) | copy-start | bytes 1540
  21.9 11.0 %copy-start.14 = (s32[64]{0:T(128)S(1)}, s32[64]{0:T(128)}, u32[]{:S(2)}) copy-start(s32[64]{0:T(128)} %param.14) | copy-start | bytes 772
  21.9 422.7 %all-to-all-start.1 = ((bf16[4,2,3,2048,256]{4,3,1,2,0:T(8,128)(2,1)}), bf16[4,2,3,2048,256]{4,3,1,2,0:T(8,128)(2,1)}, u32[]{:S(2)}, u32[]{:S(2)}) async-start(bf16[4,2,3,2048,256]{4,3,1,2,0:T(8,128)(2,1)} %stack.2), calls=%async_computation.2 | async-start | bytes 50331648 | tf_op jit(solution)/shard_map/all_to_all | solution.py:159
  30.4 295.7 %all-gather.2.cloned.1.call-start = ((), (), s32[]{:S(2)}) async-start(), calls=%async_computation.4 | async-start | bytes 1310720 | tf_op jit(solution)/shard_map/all_gather | solution.py:101
  31.5 406.4 %reduce-scatter.2.cloned.1.call-start = ((), (), s32[]{:S(2)}) async-start(), calls=%async_computation.5 | async-start | bytes 1310720 | tf_op jit(solution)/shard_map/reduce_scatter | solution.py:130
  315.9 8.9 %copy-start.12 = (s32[2]{0:T(128)S(1)}, s32[2]{0:T(128)}, u32[]{:S(2)}) copy-start(s32[2]{0:T(128)} %param.15) | copy-start | bytes 28
  315.9 9.0 %copy-start.13 = (s32[2]{0:T(128)S(1)}, s32[2]{0:T(128)}, u32[]{:S(2)}) copy-start(s32[2]{0:T(128)} %param.16) | copy-start | bytes 28
  369.0 34.8 %copy-start.7 = (bf16[256,4,64]{0,2,1:T(8,128)(2,1)S(1)}, bf16[256,4,64]{0,2,1:T(8,128)(2,1)}, u32[]{:S(2)}) copy-start(bf16[256,4,64]{0,2,1:T(8,128)(2,1)} %get-tuple-element.6) | copy-start | bytes 393220
  406.8 1.9 copy-start.2
  411.6 1.8 copy-start.8
  411.6 27.6 %copy-start.10 = (f32[2048]{0:T(1024)S(1)}, f32[2048]{0:T(1024)}, u32[]{:S(2)}) copy-start(f32[2048]{0:T(1024)} %param.22) | copy-start | bytes 24580
  444.6 61.4 %all-to-all-start = ((bf16[32,2,16,2048]{3,2,1,0:T(8,128)(2,1)}), bf16[32,2,16,2048]{3,2,1,0:T(8,128)(2,1)}, u32[]{:S(2)}, u32[]{:S(2)}) async-start(bf16[32,2,16,2048]{3,2,1,0:T(8,128)(2,1)} %bitcast.175), calls=%async_computation.1 | async-start | bytes 8388608 | tf_op jit(solution)/shard_map/all_to_all | solution.py:155
  534.3 7.4 %copy-start.11 = (f32[64,8]{0,1:T(8,128)S(1)}, f32[64,8]{0,1:T(8,128)}, u32[]{:S(2)}) copy-start(f32[64,8]{0,1:T(8,128)} %param.24) | copy-start | bytes 6148
  534.3 59.3 %all-to-all-start.2 = ((bf16[32,2,16,2048]{3,2,1,0:T(8,128)(2,1)}), bf16[32,2,16,2048]{3,2,1,0:T(8,128)(2,1)}, u32[]{:S(2)}, u32[]{:S(2)}) async-start(bf16[32,2,16,2048]{3,2,1,0:T(8,128)(2,1)} %copy.55), calls=%async_computation.3 | async-start | bytes 8388608 | tf_op jit(solution)/shard_map/all_to_all | solution.py:163
  593.6 11.6 %copy-start.5 = (bf16[64,2048]{1,0:T(8,128)(2,1)S(1)}, bf16[64,2048]{1,0:T(8,128)(2,1)}, u32[]{:S(2)}) copy-start(bf16[64,2048]{1,0:T(8,128)(2,1)} %reduce-scatter.2.cloned.1.call-done) | copy-start | bytes 786436
  593.6 12.4 %copy-start.1 = (bf16[512,2048]{1,0:T(8,128)(2,1)S(1)}, bf16[512,2048]{1,0:T(8,128)(2,1)}, u32[]{:S(2)}) copy-start(bf16[512,2048]{1,0:T(8,128)(2,1)} %param.21) | copy-start | bytes 6291460
Sparse Core Ops, SparseCore 0:
  33.5 34.1 all-gather.1
  413.5 24.4 reduce-scatter.1
